TPU v7x, 128 devices: a whole 4x4x4 slice. The times are simulated.
128 devices in a mesh: row: 16 (over x, y_lo, core), col: 8 (over y_hi, z).
Axes of the slice: x: 4, y: 4 (y_hi: 2, y_lo: 2; y = y_hi * 2 + y_lo), z: 4, core: 2. Of those that a mesh axis runs over, the one named last changes fastest.
Arguments:
- coarse_feats: bfloat16 [64, 1024], P(None, ('row', 'col')), may hold values from -6 to 6
- fine_feats: bfloat16 [64, 1024], P(None, ('row', 'col')), may hold values from -6 to 6
- pair_prior: bfloat16 [64, 1024, 1024], P(None, 'row', 'col'), may hold values from -6 to 6
- zoom_start: int32 [2], replicated, may hold values from 0 to 512, as said below
- coarse_weights: bfloat16 [2, 3, 64, 192], replicated, may hold values from -0.25 to 0.25
- coarse_bias: float32 [2, 64], replicated, may hold values from -2.5 to 2.5
- refine_first: bfloat16 [3, 64, 384], replicated, may hold values from -0.1875 to 0.1875
- refine_second: bfloat16 [3, 64, 192], replicated, may hold values from -0.25 to 0.25
- refine_bias: float32 [2, 64], replicated, may hold values from -2.5 to 2.5
Outputs:
- coarse_map: bfloat16 [64, 1024, 1024], P(None, 'row', 'col')
- refined: bfloat16 [64, 1024, 1024], P(None, 'row', 'col')
Inputs may be any that keep to these rules, and one draw needn't show every extreme that they name: `zoom_start`: the two entries are 0 and 512 in either order.
All inputs are finite; a program needn't handle non-finite values.
Results may differ from a plain program's by a relative error of at most 0.0059.
Values may be sent and summed in bfloat16 or wider, within the bound.
A program may use at most 64 MiB of HBM per device.

v0:
```python
import jax
import jax.numpy as jnp
from jax import lax
from jax.sharding import PartitionSpec as P

margin_bins = 24


def with_halo(block, sides, width):
    for axis, dim in sides:
        count = lax.axis_size(axis)
        forward = [(i, i + 1) for i in range(count - 1)]
        backward = [(target, source) for source, target in forward]
        low = lax.ppermute(
            lax.slice_in_dim(block, block.shape[dim] - width, None, axis=dim), axis, forward
        )
        high = lax.ppermute(lax.slice_in_dim(block, 0, width, axis=dim), axis, backward)
        block = jnp.concatenate([low, block, high], axis=dim)
    return block


def conv_valid(padded, weights, spacing, out_rows, out_cols):
    inputs = padded.shape[0]
    outputs = weights.shape[1]
    summed = jnp.zeros((outputs, out_rows * out_cols), jnp.float32)
    for tap_row in range(3):
        strip = padded[:, tap_row * spacing : tap_row * spacing + out_rows, :]
        slices = [
            strip[:, :, tap_col * spacing : tap_col * spacing + out_cols] for tap_col in range(3)
        ]
        if 3 * inputs <= 256:
            stacked = jnp.concatenate(slices, axis=0).reshape(3 * inputs, out_rows * out_cols)
            summed = summed + jnp.dot(weights[tap_row], stacked, preferred_element_type=jnp.float32)
        else:
            for tap_col in range(3):
                kernel = weights[tap_row][:, tap_col * inputs : (tap_col + 1) * inputs]
                summed = summed + jnp.dot(
                    kernel,
                    slices[tap_col].reshape(inputs, out_rows * out_cols),
                    preferred_element_type=jnp.float32,
                )
    return summed.reshape(outputs, out_rows, out_cols)


def conv_layer(padded, weights, biases, spacing, out_rows, out_cols):
    result = conv_valid(padded, weights, spacing, out_rows, out_cols)
    return jnp.maximum(result + biases[:, None, None], 0.0)


def pair_sum(padded_feats, row_first, col_first, row_extent, col_extent):
    row_part = lax.dynamic_slice_in_dim(
        padded_feats, row_first + margin_bins, row_extent, 1
    ).astype(jnp.float32)
    col_part = lax.dynamic_slice_in_dim(
        padded_feats, col_first + margin_bins, col_extent, 1
    ).astype(jnp.float32)
    return row_part[:, :, None] + col_part[:, None, :]


def inside_grid(row_first, col_first, row_extent, col_extent, bins_side):
    row_ids = row_first + jnp.arange(row_extent, dtype=jnp.int32)
    col_ids = col_first + jnp.arange(col_extent, dtype=jnp.int32)
    row_inside = (row_ids >= 0) & (row_ids < bins_side)
    col_inside = (col_ids >= 0) & (col_ids < bins_side)
    return (row_inside[:, None] & col_inside[None, :])[None]


def direct_move(source, axis_dim, extent, position, offset, sender):
    length = source.shape[axis_dim]
    layout = source.shape[:axis_dim] + (2, length // 2) + source.shape[axis_dim + 1 :]
    halves = jnp.moveaxis(source.reshape(layout), axis_dim, 0)
    targets = jnp.arange(extent, dtype=jnp.int32)
    owners = offset + targets // 2
    chosen = jnp.take(halves, targets % 2, axis=0)
    keeping = (owners == position).reshape((extent,) + (1,) * source.ndim)
    outgoing = jnp.where(keeping, chosen, jnp.zeros_like(chosen))
    incoming = sender(outgoing)
    return lax.dynamic_index_in_dim(incoming, offset + position // 2, 0, keepdims=False)


def per_device(
    coarse_feats,
    fine_feats,
    pair_prior,
    zoom_start,
    coarse_weights,
    coarse_bias,
    refine_first,
    refine_second,
    refine_bias,
):
    channels, tile_rows, tile_cols = pair_prior.shape
    row_count = lax.axis_size("row")
    col_count = lax.axis_size("col")
    bins_side = tile_rows * row_count
    row_place = lax.axis_index("row")
    col_place = lax.axis_index("col")
    row_start = row_place * tile_rows
    col_start = col_place * tile_cols
    coarse_all, fine_all = (
        lax.all_gather(coarse_feats, ("row", "col"), axis=1, tiled=True),
        lax.all_gather(fine_feats, ("row", "col"), axis=1, tiled=True),
    )
    coarse_padded = jnp.pad(coarse_all, ((0, 0), (margin_bins, margin_bins)))
    fine_padded = jnp.pad(fine_all, ((0, 0), (margin_bins, margin_bins)))
    pair_map = (
        pair_sum(coarse_padded, row_start, col_start, tile_rows, tile_cols)
        + pair_prior.astype(jnp.float32)
    ).astype(jnp.bfloat16)
    padded = with_halo(pair_map, (("row", 1), ("col", 2)), 2)
    hidden_coarse = conv_layer(
        padded, coarse_weights[0], coarse_bias[0], 2, tile_rows, tile_cols
    ).astype(jnp.bfloat16)
    padded = with_halo(hidden_coarse, (("row", 1), ("col", 2)), 4)
    coarse_map = conv_layer(
        padded, coarse_weights[1], coarse_bias[1], 4, tile_rows, tile_cols
    ).astype(jnp.bfloat16)
    zoom_bin = zoom_start[0]
    col_offset = zoom_bin // tile_cols
    row_offset = zoom_bin // tile_rows
    narrowed = direct_move(
        coarse_map,
        2,
        col_count,
        col_place,
        col_offset,
        lambda outgoing: lax.all_to_all(outgoing, "col", split_axis=0, concat_axis=0, tiled=True),
    )
    window = direct_move(
        narrowed,
        1,
        row_count,
        row_place,
        row_offset,
        lambda outgoing: lax.all_to_all(outgoing, "row", split_axis=0, concat_axis=0, tiled=True),
    )
    upsampled = jnp.broadcast_to(
        window[:, :, None, :, None], (channels, tile_rows // 2, 2, tile_cols // 2, 2)
    ).reshape(channels, tile_rows, tile_cols)
    window_padded = with_halo(upsampled, (("row", 1), ("col", 2)), 8)
    inside = inside_grid(row_start - 8, col_start - 8, tile_rows + 16, tile_cols + 16, bins_side)
    fine_pair = jnp.where(
        inside,
        pair_sum(fine_padded, row_start - 8, col_start - 8, tile_rows + 16, tile_cols + 16),
        0.0,
    ).astype(jnp.bfloat16)
    joined = jnp.concatenate([window_padded, fine_pair], axis=0)
    hidden_refine = conv_layer(
        joined, refine_first, refine_bias[0], 8, tile_rows, tile_cols
    ).astype(jnp.bfloat16)
    padded = with_halo(hidden_refine, (("row", 1), ("col", 2)), 16)
    refined = conv_layer(padded, refine_second, refine_bias[1], 16, tile_rows, tile_cols).astype(
        jnp.bfloat16
    )
    return (coarse_map, refined)


def solution(mesh):
    return jax.shard_map(
        per_device,
        mesh=mesh,
        in_specs=(
            P(None, ("row", "col")),
            P(None, ("row", "col")),
            P(None, "row", "col"),
            P(),
            P(),
            P(),
            P(),
            P(),
            P(),
        ),
        out_specs=(P(None, "row", "col"), P(None, "row", "col")),
        check_vma=False,
    )
```

profile of v0, /device:TPU:98, one launch (start us, length us, event | category | flops | bytes accessed | tf_op | source)
XLA Modules:
  0.0 1006.4 jit_solution(12770333739575595750)
XLA Ops:
  0.6 280.9 %all_gather.6 = bf16[64,1024]{0,1:T(8,128)(2,1)S(1)} all-gather(bf16[64,8]{0,1:T(8,128)(2,1)} %param.9), channel_id=1, replica_groups=mesh['row'=16,'col'=8] {'row','col'}, dimensions={1}, use_global_device_ids=true | all-gather | bytes 132096 | tf_op jit(solution)/shard_map/all_gather | solution.py:101
  285.9 2.4 collective-permute-start
  288.4 3.7 collective-permute-done
  294.2 7.8 collective-permute-start.2
  307.6 5.2 collective-permute-done.3
  314.7 2.2 maximum_maximum_fusion.2
  318.6 8.5 fusion.37
  329.8 5.6 collective-permute-start.5
  337.4 23.0 %collective-permute-done.4 = bf16[64,4,128]{2,0,1:T(8,128)(2,1)S(1)} collective-permute-done((bf16[64,4,128]{2,0,1:T(8,128)(2,1)S(1)}, bf16[64,4,128]{2,0,1:T(8,128)(2,1)S(1)}, u32[]{:S(2)}, u32[]{:S(2)}) %collective-permute-start.4) | collective-permute-done | bytes 65568 | tf_op jit(solution)/shard_map/ppermute | solution.py:14
  363.1 3.2 collective-permute-start.6
  367.7 2.9 collective-permute-start.7
  372.6 4.9 collective-permute-done.7
  377.6 2.9 copy.148
  380.4 2.3 maximum_maximum_fusion.1
  384.5 9.4 fusion.31
  396.1 4.4 reshape.256
  400.5 2.7 fusion.41
  403.3 4.6 gather_fusion
  407.9 7.9 select_select_fusion.1
  415.7 10.5 %reshape.289 = bf16[8,2,131072]{2,1,0:T(2,128)(2,1)} reshape(bf16[8,64,64,64]{3,2,1,0:T(8,128)(2,1)} %select_select_fusion.1) | data formatting | bytes 8388608
  426.2 5.0 all-to-all-start
  431.3 28.8 %all-to-all-done = bf16[8,2,131072]{2,1,0:T(2,128)(2,1)} async-done(((bf16[8,2,131072]{2,1,0:T(2,128)(2,1)}), bf16[8,2,131072]{2,1,0:T(2,128)(2,1)}, u32[]{:S(2)}, u32[]{:S(2)}) %all-to-all-start) | async-done | bytes 4194336 | tf_op jit(solution)/shard_map/all_to_all | solution.py:127
  460.0 10.3 %reshape.290 = bf16[8,64,64,64]{3,2,1,0:T(8,128)(2,1)} reshape(bf16[8,2,131072]{2,1,0:T(2,128)(2,1)} %all-to-all-done) | data formatting | bytes 8388608
  471.6 4.7 gather_fusion.1
  476.3 7.9 select_select_fusion
  484.2 14.0 %reshape.291 = bf16[16,2,65536]{2,1,0:T(2,128)(2,1)} reshape(bf16[16,64,32,64]{3,2,1,0:T(8,128)(2,1)} %select_select_fusion) | data formatting | bytes 8388608
  498.1 23.0 %all-to-all-start.1 = ((bf16[16,2,65536]{2,1,0:T(2,128)(2,1)}), bf16[16,2,65536]{2,1,0:T(2,128)(2,1)}, u32[]{:S(2)}, u32[]{:S(2)}) async-start(bf16[16,2,65536]{2,1,0:T(2,128)(2,1)} %reshape.291), calls=%async_computation.1 | async-start | bytes 8388608 | tf_op jit(solution)/shard_map/all_to_all | solution.py:135
  521.1 316.2 %all_gather.7 = bf16[64,1024]{0,1:T(8,128)(2,1)S(1)} all-gather(bf16[64,8]{0,1:T(8,128)(2,1)S(1)} %copy-done.11), channel_id=1, replica_groups=mesh['row'=16,'col'=8] {'row','col'}, dimensions={1}, use_global_device_ids=true | all-gather | bytes 132096 | tf_op jit(solution)/shard_map/all_gather | solution.py:102
  837.6 2.4 select_convert_fusion
  840.0 13.6 %reshape.292 = bf16[16,64,32,64]{3,2,1,0:T(8,128)(2,1)} reshape(bf16[16,2,65536]{2,1,0:T(2,128)(2,1)} %all-to-all-done.1) | data formatting | bytes 8388608
  861.1 2.4 collective-permute-start.8
  865.0 4.7 collective-permute-done.8
  869.7 2.6 collective-permute-start.11
  872.3 7.2 collective-permute-start.10
  882.3 3.9 pad_maximum_fusion.7
  886.2 5.6 fusion.97
  902.3 14.9 %collective-permute-start.13 = (bf16[64,16,128]{2,1,0:T(8,128)(2,1)S(1)}, bf16[64,16,128]{2,1,0:T(8,128)(2,1)S(1)}, u32[]{:S(2)}, u32[]{:S(2)}) collective-permute-start(bf16[64,16,128]{2,1,0:T(8,128)(2,1)S(1)} %copy.157), channel_id=1, source_target_pairs={{8,0},{16,8},{24,16},{32,24},{40,32},{48,40},{56,48},{64,56},{72,6... | collective-permute-start | bytes 786440 | tf_op jit(solution)/shard_map/ppermute | solution.py:17
  921.2 22.6 %collective-permute-done.12 = bf16[64,16,128]{2,1,0:T(8,128)(2,1)S(1)} collective-permute-done((bf16[64,16,128]{2,1,0:T(8,128)(2,1)S(1)}, bf16[64,16,128]{2,1,0:T(8,128)(2,1)S(1)}, u32[]{:S(2)}, u32[]{:S(2)}) %collective-permute-start.12) | collective-permute-done | bytes 262176 | tf_op jit(solution)/shard_map/ppermute | solution.py:14
  944.5 2.3 fusion.103
  946.8 3.4 copy.160
  950.3 7.2 collective-permute-start.14
  957.5 3.3 copy.163
  960.7 2.1 collective-permute-start.15
  964.9 3.1 copy.161
  968.1 4.9 collective-permute-done.15
  972.9 3.9 copy.164
  976.9 7.9 maximum_maximum_fusion
  986.5 15.3 %fusion.25 = (bf16[64,24,8,128]{3,2,1,0:T(8,128)(2,1)S(1)}, bf16[64,24,8,128]{3,2,1,0:T(8,128)(2,1)S(1)}, bf16[64,24,8,128]{3,2,1,0:T(8,128)(2,1)S(1)}) fusion(bf16[64,16,128]{2,0,1:T(8,128)(2,1)S(1)} %copy.159, bf16[64,64,128]{2,0,1:T(8,128)(2,1)S(1)} %fusion.45, bf16[64,64,128]{2,0,1:T(8,128)(2,1)S(1)} %get-tuple-element.15, ...), kind=kLoop, calls=%fused_computation.46 | loop fusion | flops 34603008 | bytes 17301504
  (118 shorter events, 66.4 us)
Async XLA Ops:
  0.6 287.7 %copy-start.12 = (f32[2,64]{1,0:T(2,128)S(1)}, f32[2,64]{1,0:T(2,128)}, u32[]{:S(2)}) copy-start(f32[2,64]{1,0:T(2,128)} %param.14) | copy-start | bytes 1540
  284.0 4.4 collective-permute-start.1
  285.9 6.1 collective-permute-start
  292.2 13.3 %copy-start.14 = (s32[2]{0:T(128)S(1)}, s32[2]{0:T(128)}, u32[]{:S(2)}) copy-start(s32[2]{0:T(128)} %param.12) | copy-start | bytes 28
  294.2 11.5 %collective-permute-start.2 = (bf16[64,68,2]{1,0,2:T(8,128)(2,1)S(1)}, bf16[64,68,2]{1,0,2:T(8,128)(2,1)S(1)}, u32[]{:S(2)}, u32[]{:S(2)}) collective-permute-start(bf16[64,68,2]{1,0,2:T(8,128)(2,1)S(1)} %copy.137), channel_id=1, source_target_pairs={{0,1},{1,2},{2,3},{3,4},{4,5},{5,6},{6,7},{8,9},{9,10},{10,11},{11... | collective-permute-start | bytes 52232 | tf_op jit(solution)/shard_map/ppermute | solution.py:14
  303.4 9.4 collective-permute-start.3
  318.6 8.5 copy-start.7
  329.8 7.6 collective-permute-start.5
  335.4 25.0 %collective-permute-start.4 = (bf16[64,4,128]{2,0,1:T(8,128)(2,1)S(1)}, bf16[64,4,128]{2,0,1:T(8,128)(2,1)S(1)}, u32[]{:S(2)}, u32[]{:S(2)}) collective-permute-start(bf16[64,4,128]{2,0,1:T(8,128)(2,1)S(1)} %get-tuple-element.64), channel_id=1, source_target_pairs={{0,8},{8,16},{16,24},{24,32},{32,40},{40,48},{48,56},{56,64},{64,7... | collective-permute-start | bytes 196616 | tf_op jit(solution)/shard_map/ppermute | solution.py:14
  363.1 7.5 collective-permute-start.6
  367.7 9.9 collective-permute-start.7
  384.5 9.4 copy-start.8
  396.1 4.4 copy-start
  426.2 33.8 %all-to-all-start = ((bf16[8,2,131072]{2,1,0:T(2,128)(2,1)}), bf16[8,2,131072]{2,1,0:T(2,128)(2,1)}, u32[]{:S(2)}, u32[]{:S(2)}) async-start(bf16[8,2,131072]{2,1,0:T(2,128)(2,1)} %reshape.289), calls=%async_computation | async-start | bytes 8388608 | tf_op jit(solution)/shard_map/all_to_all | solution.py:127
  498.1 23.0 %copy-start.11 = (bf16[64,8]{0,1:T(8,128)(2,1)S(1)}, bf16[64,8]{0,1:T(8,128)(2,1)}, u32[]{:S(2)}) copy-start(bf16[64,8]{0,1:T(8,128)(2,1)} %param.10) | copy-start | bytes 3076
  498.1 341.8 %all-to-all-start.1 = ((bf16[16,2,65536]{2,1,0:T(2,128)(2,1)}), bf16[16,2,65536]{2,1,0:T(2,128)(2,1)}, u32[]{:S(2)}, u32[]{:S(2)}) async-start(bf16[16,2,65536]{2,1,0:T(2,128)(2,1)} %reshape.291), calls=%async_computation.1 | async-start | bytes 8388608 | tf_op jit(solution)/shard_map/all_to_all | solution.py:135
  857.1 6.5 copy-start.9
  857.1 22.4 %copy-start.13 = (f32[2,64]{1,0:T(2,128)S(1)}, f32[2,64]{1,0:T(2,128)}, u32[]{:S(2)}) copy-start(f32[2,64]{1,0:T(2,128)} %param.17) | copy-start | bytes 1540
  859.2 5.8 collective-permute-start.9
  861.1 8.6 collective-permute-start.8
  869.7 11.1 %collective-permute-start.11 = (bf16[64,80,8]{0,2,1:T(8,128)(2,1)S(1)}, bf16[64,80,8]{0,2,1:T(8,128)(2,1)S(1)}, u32[]{:S(2)}, u32[]{:S(2)}) collective-permute-start(bf16[64,80,8]{0,2,1:T(8,128)(2,1)S(1)} %get-tuple-element.28), channel_id=1, source_target_pairs={{1,0},{2,1},{3,2},{4,3},{5,4},{6,5},{7,6},{9,8},{10,9},{11,10},{12... | collective-permute-start | bytes 245768 | tf_op jit(solution)/shard_map/ppermute | solution.py:17
  872.3 10.0 collective-permute-start.10
  891.8 1.6 copy-start.4
  893.4 1.6 copy-start.3
  895.0 1.6 copy-start.2
  902.3 18.8 %collective-permute-start.13 = (bf16[64,16,128]{2,1,0:T(8,128)(2,1)S(1)}, bf16[64,16,128]{2,1,0:T(8,128)(2,1)S(1)}, u32[]{:S(2)}, u32[]{:S(2)}) collective-permute-start(bf16[64,16,128]{2,1,0:T(8,128)(2,1)S(1)} %copy.157), channel_id=1, source_target_pairs={{8,0},{16,8},{24,16},{32,24},{40,32},{48,40},{56,48},{64,56},{72,6... | collective-permute-start | bytes 786440 | tf_op jit(solution)/shard_map/ppermute | solution.py:17
  917.4 26.3 %collective-permute-start.12 = (bf16[64,16,128]{2,1,0:T(8,128)(2,1)S(1)}, bf16[64,16,128]{2,1,0:T(8,128)(2,1)S(1)}, u32[]{:S(2)}, u32[]{:S(2)}) collective-permute-start(bf16[64,16,128]{2,1,0:T(8,128)(2,1)S(1)} %copy.156), channel_id=1, source_target_pairs={{0,8},{8,16},{16,24},{24,32},{32,40},{40,48},{48,56},{56,64},{64,7... | collective-permute-start | bytes 786440 | tf_op jit(solution)/shard_map/ppermute | solution.py:14
  943.8 0.7 copy-start.5
  946.8 16.0 %copy-start.1 = (f32[8192,64]{0,1:T(8,128)S(1)}, f32[8192,64]{0,1:T(8,128)}, u32[]{:S(2)}) copy-start(f32[8192,64]{0,1:T(8,128)} %copy-done) | copy-start | bytes 6291460
  950.3 14.7 %collective-permute-start.14 = (bf16[64,96,16]{1,2,0:T(8,128)(2,1)}, bf16[64,96,16]{1,2,0:T(8,128)(2,1)}, u32[]{:S(2)}, u32[]{:S(2)}) collective-permute-start(bf16[64,96,16]{1,2,0:T(8,128)(2,1)} %copy.160), channel_id=1, source_target_pairs={{0,1},{1,2},{2,3},{3,4},{4,5},{5,6},{6,7},{8,9},{9,10},{10,11},{11... | collective-permute-start | bytes 589832 | tf_op jit(solution)/shard_map/ppermute | solution.py:14
  960.7 12.2 %collective-permute-start.15 = (bf16[64,96,16]{1,2,0:T(8,128)(2,1)}, bf16[64,96,16]{1,2,0:T(8,128)(2,1)}, u32[]{:S(2)}, u32[]{:S(2)}) collective-permute-start(bf16[64,96,16]{1,2,0:T(8,128)(2,1)} %copy.163), channel_id=1, source_target_pairs={{1,0},{2,1},{3,2},{4,3},{5,4},{6,5},{7,6},{9,8},{10,9},{11,10},{12... | collective-permute-start | bytes 589832 | tf_op jit(solution)/shard_map/ppermute | solution.py:17
  963.3 13.6 %copy-start.6 = (bf16[64,16,128]{2,0,1:T(8,128)(2,1)S(1)}, bf16[64,16,128]{2,0,1:T(8,128)(2,1)}, u32[]{:S(2)}) copy-start(bf16[64,16,128]{2,0,1:T(8,128)(2,1)} %copy-done.5) | copy-start | bytes 786436
  986.5 15.4 %copy-start.10 = (bf16[3,64,192]{2,1,0:T(8,128)(2,1)S(1)}, bf16[3,64,192]{2,1,0:T(8,128)(2,1)}, u32[]{:S(2)}) copy-start(bf16[3,64,192]{2,1,0:T(8,128)(2,1)} %param.16) | copy-start | bytes 221188
where the time goes:
time: 1010 us
  blocking collectives  597 us (59%)
  local copies, waits for them, and re-layouts  119 us (12%)
  waiting for transfers between devices  104 us (10%)
  starting transfers between devices  95.9 us (9%)
  other arithmetic  74.8 us (7%)
  matrix products  14.3 us (1%)
    all_gather x1, blocking collectives, per_device(): lax.all_gather(fine_feats, ('row', 'col'), axis=1, tiled=True)  316 us
    all_gather x1, blocking collectives, per_device(): lax.all_gather(coarse_feats, ('row', 'col'), axis=1, tiled=True)  281 us
    ppermute x8, waiting for transfers between devices, with_halo(): lax.ppermute(lax.slice_in_dim(block, block.shape[dim] - width, None, axis...  55.5 us
    unnamed x36, local copies, waits for them, and re-layouts  54.5 us
    ppermute x8, starting transfers between devices, with_halo(): lax.ppermute(lax.slice_in_dim(block, 0, width, axis=dim), axis, backward)  34.1 us
    ppermute x8, starting transfers between devices, with_halo(): lax.ppermute(lax.slice_in_dim(block, block.shape[dim] - width, None, axis...  33.9 us
    unnamed x3, other arithmetic  33.3 us
    all_to_all x1, waiting for transfers between devices, per_device(): lax.all_to_all(outgoing, 'col', split_axis=0, concat_axis=0, tiled=True)  28.8 us
  transfers between devices with their start and end apart: 18, of which 12 were waited for; matrix products, arithmetic and copies ran while one was open for 2% of the time, Pallas kernels for 0%

commit v1 on v0

--- a/solution.py
+++ b/solution.py
@@ -99,7 +99,12 @@
     col_start = col_place * tile_cols
     coarse_all, fine_all = (
         lax.all_gather(coarse_feats, ("row", "col"), axis=1, tiled=True),
-        lax.all_gather(fine_feats, ("row", "col"), axis=1, tiled=True),
+        jnp.concatenate(
+            lax.all_to_all(
+                jnp.stack([fine_feats] * lax.axis_size(("row", "col"))), ("row", "col"), 0, 0
+            ),
+            axis=1,
+        ),
     )
     coarse_padded = jnp.pad(coarse_all, ((0, 0), (margin_bins, margin_bins)))
     fine_padded = jnp.pad(fine_all, ((0, 0), (margin_bins, margin_bins)))

time: 1010 us -> 728 us (0.72)
  blocking collectives: 597 us -> 281 us
  waiting for transfers between devices: 104 us -> 130 us
    all_gather x1 -> x0, blocking collectives: 316 us -> none  [per_device(): lax.all_gather(fine_feats, ('row', 'col'), axis=1, tiled=True)]
    all_to_all x1, waiting for transfers between devices: 0.01 us -> 48.3 us  [per_device(): lax.all_to_all(outgoing, 'row', split_axis=0, concat_axis=0, tiled=True)]
    all_to_all x0 -> x1, starting transfers between devices: none -> 23.2 us  [per_device(): lax.all_to_all(jnp.stack([fine_feats] * lax.axis_size(('row', 'col'))), (...]
    ppermute x8, waiting for transfers between devices: 55.5 us -> 36.4 us  [with_halo(): lax.ppermute(lax.slice_in_dim(block, block.shape[dim] - width, None, axis...]
    all_to_all x1, starting transfers between devices: 23 us -> 5.95 us  [per_device(): lax.all_to_all(outgoing, 'row', split_axis=0, concat_axis=0, tiled=True)]
    unnamed x36 -> x43, local copies, waits for them, and re-layouts: 54.5 us -> 55.6 us
  transfers between devices with their start and end apart: 18 -> 19, of which waited for: 12 -> 12; matrix products, arithmetic and copies ran while one was open for 2% -> 8% of each run, Pallas kernels for 0% -> 0%
where the time goes in v1:
time: 728 us; the launch traced here: 721 us
  blocking collectives  281 us (39%)
  waiting for transfers between devices  130 us (18%)
  local copies, waits for them, and re-layouts  118 us (16%)
  starting transfers between devices  99.9 us (14%)
  other arithmetic  75.3 us (10%)
  matrix products  14.3 us (2%)
    all_gather x1, blocking collectives, per_device(): lax.all_gather(coarse_feats, ('row', 'col'), axis=1, tiled=True)  281 us
    unnamed x43, local copies, waits for them, and re-layouts  55.6 us
    all_to_all x1, waiting for transfers between devices, per_device(): lax.all_to_all(outgoing, 'row', split_axis=0, concat_axis=0, tiled=True)  48.3 us
    ppermute x8, waiting for transfers between devices, with_halo(): lax.ppermute(lax.slice_in_dim(block, block.shape[dim] - width, None, axis...  36.4 us
    ppermute x8, starting transfers between devices, with_halo(): lax.ppermute(lax.slice_in_dim(block, block.shape[dim] - width, None, axis...  35 us
    unnamed x3, other arithmetic  33.3 us
    ppermute x8, starting transfers between devices, with_halo(): lax.ppermute(lax.slice_in_dim(block, 0, width, axis=dim), axis, backward)  31.2 us
    all_to_all x1, waiting for transfers between devices, per_device(): lax.all_to_all(outgoing, 'col', split_axis=0, concat_axis=0, tiled=True)  27.9 us
  transfers between devices with their start and end apart: 19, of which 12 were waited for; matrix products, arithmetic and copies ran while one was open for 8% of the time, Pallas kernels for 0%

profile of v1, /device:TPU:98, one launch (start us, length us, event | category | flops | bytes accessed | tf_op | source)
XLA Modules:
  0.0 720.7 jit_solution(7416161322257989349)
XLA Ops:
  0.7 280.9 %all_gather.3 = bf16[64,1024]{0,1:T(8,128)(2,1)S(1)} all-gather(bf16[64,8]{0,1:T(8,128)(2,1)} %param.9), channel_id=1, replica_groups=mesh['row'=16,'col'=8] {'row','col'}, dimensions={1}, use_global_device_ids=true | all-gather | bytes 132096 | tf_op jit(solution)/shard_map/all_gather | solution.py:101
  286.0 2.4 collective-permute-start
  288.4 3.7 collective-permute-done
  294.2 7.8 %collective-permute-start.2 = (bf16[64,68,2]{1,0,2:T(8,128)(2,1)S(1)}, bf16[64,68,2]{1,0,2:T(8,128)(2,1)S(1)}, u32[]{:S(2)}, u32[]{:S(2)}) collective-permute-start(bf16[64,68,2]{1,0,2:T(8,128)(2,1)S(1)} %copy.136), channel_id=1, source_target_pairs={{0,1},{1,2},{2,3},{3,4},{4,5},{5,6},{6,7},{8,9},{9,10},{10,11},{11... | collective-permute-start | bytes 52232 | tf_op jit(solution)/shard_map/ppermute | solution.py:14
  307.6 5.2 collective-permute-done.3
  314.7 2.3 maximum_maximum_fusion.2
  318.7 8.5 %fusion.37 = (bf16[64,24,8,128]{3,2,1,0:T(8,128)(2,1)S(1)}, bf16[64,24,8,128]{3,2,1,0:T(8,128)(2,1)S(1)}, bf16[64,24,8,128]{3,2,1,0:T(8,128)(2,1)S(1)}) fusion(bf16[64,2,128]{2,0,1:T(8,128)(2,1)S(1)} %collective-permute-done.1, bf16[64,64,128]{2,0,1:T(8,128)(2,1)S(1)} %add_convert_fusion, bf16[64,64,128]{2,0,1:T(8,128)(2,1)S(1)} %get-tuple-element.83, ...), kind=kLoop, calls=%fused_computation.62 | loop fusion | flops 34603008 | bytes 16842752
  329.8 5.6 collective-permute-start.5
  337.4 23.0 %collective-permute-done.4 = bf16[64,4,128]{2,0,1:T(8,128)(2,1)S(1)} collective-permute-done((bf16[64,4,128]{2,0,1:T(8,128)(2,1)S(1)}, bf16[64,4,128]{2,0,1:T(8,128)(2,1)S(1)}, u32[]{:S(2)}, u32[]{:S(2)}) %collective-permute-start.4) | collective-permute-done | bytes 65568 | tf_op jit(solution)/shard_map/ppermute | solution.py:14
  363.2 3.4 collective-permute-start.6
  368.0 2.8 collective-permute-start.7
  373.4 4.5 collective-permute-done.7
  377.8 2.9 copy.147
  380.7 2.3 maximum_maximum_fusion.1
  384.8 9.4 %fusion.31 = (bf16[64,24,8,128]{3,2,1,0:T(8,128)(2,1)S(1)}, bf16[64,24,8,128]{3,2,1,0:T(8,128)(2,1)S(1)}, bf16[64,24,8,128]{3,2,1,0:T(8,128)(2,1)S(1)}) fusion(bf16[64,4,128]{2,0,1:T(8,128)(2,1)S(1)} %collective-permute-done.5, bf16[64,64,128]{2,0,1:T(8,128)(2,1)S(1)} %fusion.49, bf16[64,64,128]{2,0,1:T(8,128)(2,1)S(1)} %get-tuple-element.32, ...), kind=kLoop, calls=%fused_computation.54 | loop fusion | flops 34603008 | bytes 16908288
  396.4 4.4 reshape.264
  400.9 2.7 fusion.41
  403.6 4.6 gather_fusion
  408.2 7.8 %select_select_fusion.1 = bf16[8,64,64,64]{3,2,1,0:T(8,128)(2,1)} fusion(bf16[8,64,64,64]{3,2,1,0:T(8,128)(2,1)} %gather_fusion, pred[8]{0:T(512)(128)(4,1)S(1)} %get-tuple-element.77, pred[8]{0:T(512)(128)(4,1)S(1)} %copy-done.13), kind=kLoop, calls=%fused_computation.17 | loop fusion | flops 4194304 | bytes 8388624 | tf_op jit(solution)/shard_map/jit(_where)/select_n | solution.py:76
  416.0 10.5 %reshape.301 = bf16[8,2,131072]{2,1,0:T(2,128)(2,1)} reshape(bf16[8,64,64,64]{3,2,1,0:T(8,128)(2,1)} %select_select_fusion.1) | data formatting | bytes 8388608
  426.5 4.5 all-to-all-start
  432.0 27.9 %all-to-all-done = bf16[8,2,131072]{2,1,0:T(2,128)(2,1)} async-done(((bf16[8,2,131072]{2,1,0:T(2,128)(2,1)}), bf16[8,2,131072]{2,1,0:T(2,128)(2,1)}, u32[]{:S(2)}, u32[]{:S(2)}) %all-to-all-start) | async-done | bytes 4194336 | tf_op jit(solution)/shard_map/all_to_all | solution.py:132
  459.9 23.2 %all-to-all-start.2 = ((bf16[128,2,256]{2,1,0:T(2,128)(2,1)}), bf16[128,2,256]{2,1,0:T(2,128)(2,1)S(1)}, u32[]{:S(2)}, u32[]{:S(2)}) async-start(bf16[128,2,256]{2,1,0:T(2,128)(2,1)} %reshape.299), calls=%async_computation.2 | async-start | bytes 262144 | tf_op jit(solution)/shard_map/all_to_all | solution.py:103
  483.2 10.3 %reshape.302 = bf16[8,64,64,64]{3,2,1,0:T(8,128)(2,1)} reshape(bf16[8,2,131072]{2,1,0:T(2,128)(2,1)} %all-to-all-done) | data formatting | bytes 8388608
  494.8 4.7 gather_fusion.1
  499.4 7.8 %select_select_fusion = bf16[16,64,32,64]{3,2,1,0:T(8,128)(2,1)} fusion(bf16[16,64,32,64]{3,2,1,0:T(8,128)(2,1)} %gather_fusion.1, pred[16]{0:T(512)(128)(4,1)S(1)} %get-tuple-element.79, pred[16]{0:T(512)(128)(4,1)S(1)} %get-tuple-element.80), kind=kLoop, calls=%fused_computation.16 | loop fusion | flops 4194304 | bytes 8388640 | tf_op jit(solution)/shard_map/jit(_where)/select_n | solution.py:76
  507.3 14.0 %reshape.303 = bf16[16,2,65536]{2,1,0:T(2,128)(2,1)} reshape(bf16[16,64,32,64]{3,2,1,0:T(8,128)(2,1)} %select_select_fusion) | data formatting | bytes 8388608
  521.2 5.9 all-to-all-start.1
  527.6 48.3 %all-to-all-done.1 = bf16[16,2,65536]{2,1,0:T(2,128)(2,1)} async-done(((bf16[16,2,65536]{2,1,0:T(2,128)(2,1)}), bf16[16,2,65536]{2,1,0:T(2,128)(2,1)}, u32[]{:S(2)}, u32[]{:S(2)}) %all-to-all-start.1) | async-done | bytes 4194336 | tf_op jit(solution)/shard_map/all_to_all | solution.py:140
  575.9 13.6 %reshape.304 = bf16[16,64,32,64]{3,2,1,0:T(8,128)(2,1)} reshape(bf16[16,2,65536]{2,1,0:T(2,128)(2,1)} %all-to-all-done.1) | data formatting | bytes 8388608
  593.3 12.1 %collective-permute-start.9 = (bf16[64,8,128]{0,2,1:T(8,128)(2,1)S(1)}, bf16[64,8,128]{0,2,1:T(8,128)(2,1)S(1)}, u32[]{:S(2)}, u32[]{:S(2)}) collective-permute-start(bf16[64,8,128]{0,2,1:T(8,128)(2,1)S(1)} %get-tuple-element.42), channel_id=1, source_target_pairs={{8,0},{16,8},{24,16},{32,24},{40,32},{48,40},{56,48},{64,56},{72,6... | collective-permute-start | bytes 393224 | tf_op jit(solution)/shard_map/ppermute | solution.py:17
  609.3 4.7 collective-permute-done.8
  614.0 2.5 collective-permute-start.11
  616.5 7.2 collective-permute-start.10
  623.7 2.4 select_convert_fusion
  626.3 3.7 pad_maximum_fusion.7
  630.0 5.6 fusion.97
  648.3 2.4 collective-permute-start.12
  652.0 4.8 collective-permute-done.12
  657.6 2.3 fusion.103
  660.0 3.4 copy.159
  663.4 8.0 %collective-permute-start.14 = (bf16[64,96,16]{1,2,0:T(8,128)(2,1)}, bf16[64,96,16]{1,2,0:T(8,128)(2,1)}, u32[]{:S(2)}, u32[]{:S(2)}) collective-permute-start(bf16[64,96,16]{1,2,0:T(8,128)(2,1)} %copy.159), channel_id=1, source_target_pairs={{0,1},{1,2},{2,3},{3,4},{4,5},{5,6},{6,7},{8,9},{9,10},{10,11},{11... | collective-permute-start | bytes 589832 | tf_op jit(solution)/shard_map/ppermute | solution.py:14
  671.4 3.3 copy.162
  678.9 3.1 copy.160
  682.1 4.8 collective-permute-done.15
  686.9 3.9 copy.163
  690.8 8.0 %maximum_maximum_fusion = (bf16[64,96,144]{2,0,1:T(8,128)(2,1)S(1)}, bf16[64,96,144]{2,0,1:T(8,128)(2,1)S(1)}) fusion(bf16[64,16,128]{2,0,1:T(8,128)(2,1)S(1)} %copy.158, bf16[64,64,128]{2,0,1:T(8,128)(2,1)S(1)} %fusion.45, bf16[64,16,128]{2,0,1:T(8,128)(2,1)S(1)} %copy-done.8, bf16[64,96,16]{2,0,1:T(8,128)(2,1)S(1)} %copy.160, bf16[64,96,16]{2,0,1:T(8,128)(2,1)} %copy.163), kind=kLoop, calls=%fused_computation.69 | loop fusion | flops 14155776 | bytes 5505024 | tf_op jit(solution)/shard_map/concatenate | solution.py:18
  700.6 15.4 %fusion.25 = (bf16[64,24,8,128]{3,2,1,0:T(8,128)(2,1)S(1)}, bf16[64,24,8,128]{3,2,1,0:T(8,128)(2,1)S(1)}, bf16[64,24,8,128]{3,2,1,0:T(8,128)(2,1)S(1)}) fusion(bf16[64,16,128]{2,0,1:T(8,128)(2,1)S(1)} %copy.158, bf16[64,64,128]{2,0,1:T(8,128)(2,1)S(1)} %fusion.45, bf16[64,64,128]{2,0,1:T(8,128)(2,1)S(1)} %get-tuple-element.15, ...), kind=kLoop, calls=%fused_computation.46 | loop fusion | flops 34603008 | bytes 17301504
  (127 shorter events, 65.9 us)
Async XLA Ops:
  0.6 430.4 %copy-start = (bf16[64,8]{0,1:T(8,128)(2,1)S(1)}, bf16[64,8]{0,1:T(8,128)(2,1)}, u32[]{:S(2)}) copy-start(bf16[64,8]{0,1:T(8,128)(2,1)} %param.10) | copy-start | bytes 3076
  0.6 287.7 %copy-start.14 = (f32[2,64]{1,0:T(2,128)S(1)}, f32[2,64]{1,0:T(2,128)}, u32[]{:S(2)}) copy-start(f32[2,64]{1,0:T(2,128)} %param.14) | copy-start | bytes 1540
  284.0 4.4 collective-permute-start.1
  286.0 6.1 collective-permute-start
  292.3 13.3 %copy-start.16 = (s32[2]{0:T(128)S(1)}, s32[2]{0:T(128)}, u32[]{:S(2)}) copy-start(s32[2]{0:T(128)} %param.12) | copy-start | bytes 28
  294.2 11.5 %collective-permute-start.2 = (bf16[64,68,2]{1,0,2:T(8,128)(2,1)S(1)}, bf16[64,68,2]{1,0,2:T(8,128)(2,1)S(1)}, u32[]{:S(2)}, u32[]{:S(2)}) collective-permute-start(bf16[64,68,2]{1,0,2:T(8,128)(2,1)S(1)} %copy.136), channel_id=1, source_target_pairs={{0,1},{1,2},{2,3},{3,4},{4,5},{5,6},{6,7},{8,9},{9,10},{10,11},{11... | collective-permute-start | bytes 52232 | tf_op jit(solution)/shard_map/ppermute | solution.py:14
  303.4 9.4 %collective-permute-start.3 = (bf16[64,68,2]{1,0,2:T(8,128)(2,1)S(1)}, bf16[64,68,2]{1,0,2:T(8,128)(2,1)S(1)}, u32[]{:S(2)}, u32[]{:S(2)}) collective-permute-start(bf16[64,68,2]{1,0,2:T(8,128)(2,1)S(1)} %copy.138), channel_id=1, source_target_pairs={{1,0},{2,1},{3,2},{4,3},{5,4},{6,5},{7,6},{9,8},{10,9},{11,10},{12... | collective-permute-start | bytes 52232 | tf_op jit(solution)/shard_map/ppermute | solution.py:17
  318.7 8.5 %copy-start.9 = (bf16[2,3,64,192]{3,2,1,0:T(8,128)(2,1)S(1)}, bf16[2,3,64,192]{3,2,1,0:T(8,128)(2,1)}, u32[]{:S(2)}) copy-start(bf16[2,3,64,192]{3,2,1,0:T(8,128)(2,1)} %param.13) | copy-start | bytes 442372
  329.8 7.6 %collective-permute-start.5 = (bf16[64,4,128]{2,0,1:T(8,128)(2,1)S(1)}, bf16[64,4,128]{2,0,1:T(8,128)(2,1)S(1)}, u32[]{:S(2)}, u32[]{:S(2)}) collective-permute-start(bf16[64,4,128]{2,0,1:T(8,128)(2,1)S(1)} %get-tuple-element.63), channel_id=1, source_target_pairs={{8,0},{16,8},{24,16},{32,24},{40,32},{48,40},{56,48},{64,56},{72,6... | collective-permute-start | bytes 196616 | tf_op jit(solution)/shard_map/ppermute | solution.py:17
  335.5 25.0 %collective-permute-start.4 = (bf16[64,4,128]{2,0,1:T(8,128)(2,1)S(1)}, bf16[64,4,128]{2,0,1:T(8,128)(2,1)S(1)}, u32[]{:S(2)}, u32[]{:S(2)}) collective-permute-start(bf16[64,4,128]{2,0,1:T(8,128)(2,1)S(1)} %get-tuple-element.64), channel_id=1, source_target_pairs={{0,8},{8,16},{16,24},{24,32},{32,40},{40,48},{48,56},{56,64},{64,7... | collective-permute-start | bytes 196616 | tf_op jit(solution)/shard_map/ppermute | solution.py:14
  363.2 8.2 %collective-permute-start.6 = (bf16[64,72,4]{1,0,2:T(8,128)(2,1)}, bf16[64,72,4]{1,0,2:T(8,128)(2,1)S(1)}, u32[]{:S(2)}, u32[]{:S(2)}) collective-permute-start(bf16[64,72,4]{1,0,2:T(8,128)(2,1)} %copy.144), channel_id=1, source_target_pairs={{0,1},{1,2},{2,3},{3,4},{4,5},{5,6},{6,7},{8,9},{9,10},{10,11},{11... | collective-permute-start | bytes 110600 | tf_op jit(solution)/shard_map/ppermute | solution.py:14
  368.0 9.9 %collective-permute-start.7 = (bf16[64,72,4]{1,0,2:T(8,128)(2,1)S(1)}, bf16[64,72,4]{1,0,2:T(8,128)(2,1)}, u32[]{:S(2)}, u32[]{:S(2)}) collective-permute-start(bf16[64,72,4]{1,0,2:T(8,128)(2,1)S(1)} %copy.146), channel_id=1, source_target_pairs={{1,0},{2,1},{3,2},{4,3},{5,4},{6,5},{7,6},{9,8},{10,9},{11,10},{12... | collective-permute-start | bytes 110600 | tf_op jit(solution)/shard_map/ppermute | solution.py:17
  384.8 9.4 %copy-start.10 = (bf16[2,3,64,192]{3,2,1,0:T(8,128)(2,1)S(1)}, bf16[2,3,64,192]{3,2,1,0:T(8,128)(2,1)}, u32[]{:S(2)}) copy-start(bf16[2,3,64,192]{3,2,1,0:T(8,128)(2,1)} %param.13) | copy-start | bytes 442372
  396.4 4.4 copy-start.2
  403.6 4.6 copy-start.13
  426.5 33.4 %all-to-all-start = ((bf16[8,2,131072]{2,1,0:T(2,128)(2,1)}), bf16[8,2,131072]{2,1,0:T(2,128)(2,1)}, u32[]{:S(2)}, u32[]{:S(2)}) async-start(bf16[8,2,131072]{2,1,0:T(2,128)(2,1)} %reshape.301), calls=%async_computation | async-start | bytes 8388608 | tf_op jit(solution)/shard_map/all_to_all | solution.py:132
  459.9 61.3 %all-to-all-start.2 = ((bf16[128,2,256]{2,1,0:T(2,128)(2,1)}), bf16[128,2,256]{2,1,0:T(2,128)(2,1)S(1)}, u32[]{:S(2)}, u32[]{:S(2)}) async-start(bf16[128,2,256]{2,1,0:T(2,128)(2,1)} %reshape.299), calls=%async_computation.2 | async-start | bytes 262144 | tf_op jit(solution)/shard_map/all_to_all | solution.py:103
  521.2 6.0 copy-start.15
  521.2 6.1 copy-start.11
  521.2 54.7 %all-to-all-start.1 = ((bf16[16,2,65536]{2,1,0:T(2,128)(2,1)}), bf16[16,2,65536]{2,1,0:T(2,128)(2,1)}, u32[]{:S(2)}, u32[]{:S(2)}) async-start(bf16[16,2,65536]{2,1,0:T(2,128)(2,1)} %reshape.303), calls=%async_computation.1 | async-start | bytes 8388608 | tf_op jit(solution)/shard_map/all_to_all | solution.py:140
  593.3 16.0 %collective-permute-start.9 = (bf16[64,8,128]{0,2,1:T(8,128)(2,1)S(1)}, bf16[64,8,128]{0,2,1:T(8,128)(2,1)S(1)}, u32[]{:S(2)}, u32[]{:S(2)}) collective-permute-start(bf16[64,8,128]{0,2,1:T(8,128)(2,1)S(1)} %get-tuple-element.42), channel_id=1, source_target_pairs={{8,0},{16,8},{24,16},{32,24},{40,32},{48,40},{56,48},{64,56},{72,6... | collective-permute-start | bytes 393224 | tf_op jit(solution)/shard_map/ppermute | solution.py:17
  605.4 8.6 %collective-permute-start.8 = (bf16[64,8,128]{0,2,1:T(8,128)(2,1)S(1)}, bf16[64,8,128]{0,2,1:T(8,128)(2,1)S(1)}, u32[]{:S(2)}, u32[]{:S(2)}) collective-permute-start(bf16[64,8,128]{0,2,1:T(8,128)(2,1)S(1)} %get-tuple-element.41), channel_id=1, source_target_pairs={{0,8},{8,16},{16,24},{24,32},{32,40},{40,48},{48,56},{56,64},{64,7... | collective-permute-start | bytes 393224 | tf_op jit(solution)/shard_map/ppermute | solution.py:14
  614.0 12.1 %collective-permute-start.11 = (bf16[64,80,8]{0,2,1:T(8,128)(2,1)S(1)}, bf16[64,80,8]{0,2,1:T(8,128)(2,1)S(1)}, u32[]{:S(2)}, u32[]{:S(2)}) collective-permute-start(bf16[64,80,8]{0,2,1:T(8,128)(2,1)S(1)} %get-tuple-element.28), channel_id=1, source_target_pairs={{1,0},{2,1},{3,2},{4,3},{5,4},{6,5},{7,6},{9,8},{10,9},{11,10},{12... | collective-permute-start | bytes 245768 | tf_op jit(solution)/shard_map/ppermute | solution.py:17
  616.5 9.8 %collective-permute-start.10 = (bf16[64,80,8]{0,2,1:T(8,128)(2,1)S(1)}, bf16[64,80,8]{0,2,1:T(8,128)(2,1)S(1)}, u32[]{:S(2)}, u32[]{:S(2)}) collective-permute-start(bf16[64,80,8]{0,2,1:T(8,128)(2,1)S(1)} %get-tuple-element.27), channel_id=1, source_target_pairs={{0,1},{1,2},{2,3},{3,4},{4,5},{5,6},{6,7},{8,9},{9,10},{10,11},{11... | collective-permute-start | bytes 245768 | tf_op jit(solution)/shard_map/ppermute | solution.py:14
  635.6 1.6 copy-start.6
  637.2 1.6 copy-start.5
  638.8 1.6 copy-start.4
  646.2 5.8 collective-permute-start.13
  648.3 8.6 %collective-permute-start.12 = (bf16[64,16,128]{2,1,0:T(8,128)(2,1)S(1)}, bf16[64,16,128]{2,1,0:T(8,128)(2,1)S(1)}, u32[]{:S(2)}, u32[]{:S(2)}) collective-permute-start(bf16[64,16,128]{2,1,0:T(8,128)(2,1)S(1)} %copy.155), channel_id=1, source_target_pairs={{0,8},{8,16},{16,24},{24,32},{32,40},{40,48},{48,56},{56,64},{64,7... | collective-permute-start | bytes 786440 | tf_op jit(solution)/shard_map/ppermute | solution.py:14
  656.9 0.7 copy-start.7
  660.0 16.9 %copy-start.3 = (f32[8192,64]{0,1:T(8,128)S(1)}, f32[8192,64]{0,1:T(8,128)}, u32[]{:S(2)}) copy-start(f32[8192,64]{0,1:T(8,128)} %copy-done.2) | copy-start | bytes 6291460
  663.4 15.5 %collective-permute-start.14 = (bf16[64,96,16]{1,2,0:T(8,128)(2,1)}, bf16[64,96,16]{1,2,0:T(8,128)(2,1)}, u32[]{:S(2)}, u32[]{:S(2)}) collective-permute-start(bf16[64,96,16]{1,2,0:T(8,128)(2,1)} %copy.159), channel_id=1, source_target_pairs={{0,1},{1,2},{2,3},{3,4},{4,5},{5,6},{6,7},{8,9},{9,10},{10,11},{11... | collective-permute-start | bytes 589832 | tf_op jit(solution)/shard_map/ppermute | solution.py:14
  674.7 12.2 %collective-permute-start.15 = (bf16[64,96,16]{1,2,0:T(8,128)(2,1)}, bf16[64,96,16]{1,2,0:T(8,128)(2,1)}, u32[]{:S(2)}, u32[]{:S(2)}) collective-permute-start(bf16[64,96,16]{1,2,0:T(8,128)(2,1)} %copy.162), channel_id=1, source_target_pairs={{1,0},{2,1},{3,2},{4,3},{5,4},{6,5},{7,6},{9,8},{10,9},{11,10},{12... | collective-permute-start | bytes 589832 | tf_op jit(solution)/shard_map/ppermute | solution.py:17
  677.2 13.6 %copy-start.8 = (bf16[64,16,128]{2,0,1:T(8,128)(2,1)S(1)}, bf16[64,16,128]{2,0,1:T(8,128)(2,1)}, u32[]{:S(2)}) copy-start(bf16[64,16,128]{2,0,1:T(8,128)(2,1)} %copy-done.7) | copy-start | bytes 786436
  700.5 15.4 %copy-start.12 = (bf16[3,64,192]{2,1,0:T(8,128)(2,1)S(1)}, bf16[3,64,192]{2,1,0:T(8,128)(2,1)}, u32[]{:S(2)}) copy-start(bf16[3,64,192]{2,1,0:T(8,128)(2,1)} %param.16) | copy-start | bytes 221188
  717.4 2.8 copy-start.1
